TPU v7x, 128 devices: a whole 4x4x4 slice. The times are simulated.
128 devices in a mesh: seq: 16 (over z, y_hi, core), col: 4 (over x), batch: 2 (over y_lo).
Axes of the slice: x: 4, y: 4 (y_hi: 2, y_lo: 2; y = y_hi * 2 + y_lo), z: 4, core: 2. Of those that a mesh axis runs over, the one named last changes fastest.
Arguments:
- tokens: int32 [2, 1048576], P('batch', ('seq', 'col')), may hold values from 0 to 3
- stem_weight: bfloat16 [64, 768], replicated, may hold values from -1.5 to 1.5
- conv_weight: bfloat16 [3840, 768], replicated, may hold values from -0.09375 to 0.09375
- conv_bias: float32 [768], replicated, may hold values from -1 to 1
- up_weight: bfloat16 [768, 1536], replicated, may hold values from -0.21875 to 0.21875
- norm_gain: float32 [1536], replicated, may hold values from 0.1 to 1.9
- pair_weight: bfloat16 [1536, 64], replicated, may hold values from -0.15625 to 0.15625
- out_weight: bfloat16 [1024, 128], replicated, may hold values from -0.1875 to 0.1875
- cotangent: bfloat16 [2, 512, 512, 128], P('batch', 'seq', 'col'), may hold values from -24 to 24
- projection: float32 [768, 128], replicated, may hold values from -0.21875 to 0.21875
- buckets: int32 [3840], replicated, may hold values from 0 to 31
Outputs:
- input_grad: bfloat16 [2, 65536, 768], P('batch', ('seq', 'col'))
- embedding: float32 [2, 32, 128], P('batch')
All inputs are finite; a program needn't handle non-finite values.
Results may differ from a plain program's by a relative error of at most 0.012.
Values may be sent and summed in bfloat16 or wider, within the bound.
No kernel may reach another device: no remote copies, remote signals or barrier semaphores. Data moves between devices by JAX's collectives and lax.ppermute only.
A program may use at most 128 MiB of HBM per device.

v0:
```python
import jax
import jax.numpy as jnp
from jax import lax
from jax.sharding import PartitionSpec as P

OP = 32
PATCH = 16
POOL = 128
BUCKETS = 32
highest = lax.Precision.HIGHEST


def extended(cells, sides, width):
    for axis, dim in sides:
        count = lax.axis_size(axis)
        ends = count - 1
        head = lax.slice_in_dim(cells, 0, width, axis=dim)
        tail = lax.slice_in_dim(cells, cells.shape[dim] - width, cells.shape[dim], axis=dim)
        cells = jnp.concatenate(
            [
                lax.ppermute(tail, axis, [(i, (i + 1) % count) for i in range(ends)]),
                cells,
                lax.ppermute(head, axis, [((i + 1) % count, i) for i in range(ends)]),
            ],
            axis=dim,
        )
    return cells


def shards(
    tokens,
    stem_weight,
    conv_weight,
    conv_bias,
    up_weight,
    norm_gain,
    pair_weight,
    out_weight,
    cotangent,
    projection,
    buckets,
):
    channels = conv_weight.shape[1]
    kernel = conv_weight.shape[0] // channels
    reach = (kernel - 1) // 2
    patches = tokens.shape[1] // PATCH
    bins_dev = patches // POOL
    bases = tokens[0].reshape(patches, PATCH)
    onehot = (
        (bases[:, :, None] == jnp.arange(4, dtype=jnp.int32))
        .astype(jnp.bfloat16)
        .reshape(patches, PATCH * 4)
    )
    embedded = jnp.dot(onehot, stem_weight, preferred_element_type=jnp.float32).astype(jnp.bfloat16)
    padded = extended(embedded, ((("seq", "col"), 0),), reach)
    unfolded = jnp.concatenate(
        [padded[offset : offset + patches] for offset in range(kernel)], axis=1
    )
    before = jnp.dot(unfolded, conv_weight, preferred_element_type=jnp.float32) + conv_bias
    after, gelu_back = jax.vjp(jax.nn.gelu, before)
    pooled = jnp.mean(after.reshape(bins_dev, POOL, channels), axis=1).astype(jnp.bfloat16)
    hidden = jnp.dot(pooled, up_weight, preferred_element_type=jnp.float32)
    inverse = lax.rsqrt(jnp.mean(hidden * hidden, axis=1, keepdims=True) + 1e-06)
    normed = (hidden * inverse * norm_gain).astype(jnp.bfloat16)
    seq_count = lax.axis_size("seq")
    col_count = lax.axis_size("col")
    row_len = bins_dev * col_count
    col_len = bins_dev * seq_count
    all_bins = row_len * seq_count
    row_index = lax.axis_index("seq")
    col_index = lax.axis_index("col")
    every = lax.all_gather(normed, ("seq", "col"), axis=0, tiled=True)
    row_part = lax.dynamic_slice_in_dim(every, row_index * row_len, row_len, 0)
    col_part = lax.dynamic_slice_in_dim(every, col_index * col_len, col_len, 0)
    left = jnp.dot(row_part, pair_weight[:, :OP], preferred_element_type=jnp.float32).astype(
        jnp.bfloat16
    )
    right = jnp.dot(col_part, pair_weight[:, OP:], preferred_element_type=jnp.float32).astype(
        jnp.bfloat16
    )
    pair_channels = cotangent.shape[3]
    blocks = cotangent[0].reshape(col_count, bins_dev, col_len, pair_channels)
    left_groups = left.astype(jnp.float32).reshape(col_count, bins_dev, OP)
    right_wide = right.astype(jnp.float32)

    def pair_step(carry, inputs):
        block, rows_left = inputs
        outer_grad = lax.dot_general(
            block.reshape(bins_dev * col_len, pair_channels),
            out_weight,
            (((1,), (1,)), ((), ())),
            preferred_element_type=jnp.float32,
        ).reshape(bins_dev, col_len, OP, OP)
        grad_left = jnp.einsum("ijkl,jl->ik", outer_grad, right_wide, precision=highest)
        carry = carry + jnp.einsum("ijkl,ik->jl", outer_grad, rows_left, precision=highest)
        return (carry, grad_left)

    grad_right, grad_left = lax.scan(
        pair_step, jnp.zeros((col_len, OP), jnp.float32), (blocks, left_groups)
    )
    grad_left = grad_left.reshape(row_len, OP)
    row_term = lax.dot_general(
        grad_left,
        pair_weight[:, :OP].astype(jnp.float32),
        (((1,), (1,)), ((), ())),
        precision=highest,
    )
    col_term = lax.dot_general(
        grad_right,
        pair_weight[:, OP:].astype(jnp.float32),
        (((1,), (1,)), ((), ())),
        precision=highest,
    )
    empty_rows = jnp.zeros((all_bins, row_term.shape[1]), jnp.float32)
    placed = lax.dynamic_update_slice_in_dim(
        empty_rows, row_term, row_index * row_len, 0
    ) + lax.dynamic_update_slice_in_dim(empty_rows, col_term, col_index * col_len, 0)
    d_normed = lax.psum_scatter(placed, ("seq", "col"), scatter_dimension=0, tiled=True)
    scaled = d_normed * norm_gain
    inner = jnp.mean(scaled * hidden, axis=1, keepdims=True)
    d_hidden = inverse * scaled - hidden * inverse**3 * inner
    d_pooled = lax.dot_general(
        d_hidden, up_weight.astype(jnp.float32), (((1,), (1,)), ((), ())), precision=highest
    )
    spread = jnp.broadcast_to(d_pooled[:, None, :] / POOL, (bins_dev, POOL, channels)).reshape(
        patches, channels
    )
    d_before = gelu_back(spread)[0].astype(jnp.bfloat16)
    grads_padded = extended(d_before, ((("seq", "col"), 0),), reach)
    stacked = jnp.stack(
        [
            grads_padded[2 * reach - offset : 2 * reach - offset + patches]
            for offset in range(kernel)
        ],
        axis=1,
    )
    input_grad = jnp.einsum(
        "tko,kio->ti",
        stacked,
        conv_weight.reshape(kernel, channels, channels),
        preferred_element_type=jnp.float32,
    ).astype(jnp.bfloat16)
    share_rows = unfolded.shape[1] // lax.axis_size(("seq", "col"))
    share = lax.psum_scatter(
        lax.dot_general(
            unfolded, d_before, (((0,), (0,)), ((), ())), preferred_element_type=jnp.float32
        ),
        ("seq", "col"),
        scatter_dimension=0,
        tiled=True,
    )
    labels = lax.dynamic_slice_in_dim(
        buckets, lax.axis_index(("seq", "col")) * share_rows, share_rows, 0
    )
    projected = jnp.dot(share, projection, precision=highest)
    member = (labels[None, :] == jnp.arange(BUCKETS, dtype=jnp.int32)[:, None]).astype(jnp.float32)
    sketch = lax.psum(jnp.dot(member, projected, precision=highest), ("seq", "col"))
    unit = sketch * lax.rsqrt(jnp.mean(sketch * sketch) + 1e-06)
    center = lax.psum(unit, "batch") / lax.axis_size("batch")
    return (input_grad[None], (unit - center)[None])


def solution(mesh):
    in_specs = (
        P("batch", ("seq", "col")),
        P(),
        P(),
        P(),
        P(),
        P(),
        P(),
        P(),
        P("batch", "seq", "col", None),
        P(),
        P(),
    )
    out_specs = (P("batch", ("seq", "col"), None), P("batch", None, None))
    return jax.shard_map(shards, mesh=mesh, in_specs=in_specs, out_specs=out_specs, check_vma=False)
```

profile of v0, /device:TPU:8, one launch (start us, length us, event | category | flops | bytes accessed | tf_op | source)
XLA Modules:
  0.0 925.7 jit_solution(1880735338173199356)
XLA Ops:
  7.7 1.8 reduce.3
  10.2 1.6 convolution_convert_fusion
  11.8 3.4 collective-permute-start
  15.2 1.3 collective-permute-start.1
  17.4 3.3 collective-permute-done.1
  21.5 8.4 bitcast_reduce_fusion
  30.4 0.7 multiply_convert_fusion
  31.4 72.0 %all-gather.2.cloned.1.call-done = bf16[512,1536]{1,0:T(8,128)(2,1)} async-done(((bf16[8,1536]{1,0:T(8,128)(2,1)}), bf16[512,1536]{1,0:T(8,128)(2,1)}) %all-gather.2.cloned.1.call-update) | async-done | bytes 1572880 | tf_op jit(solution)/shard_map/all_gather | solution.py:72
  103.4 1.2 fusion.37
  104.8 1.0 fusion.39
  105.8 78.4 %while.13 = (s32[]{:T(128)}, f32[128,32]{1,0:T(8,128)S(1)}, f32[4,8,32]{2,1,0:T(8,128)S(1)}, bf16[4,8,128,128]{3,2,1,0:T(8,128)(2,1)}, bf16[1024,128]{1,0:T(8,12...) while((s32[]{:T(128)}, f32[128,32]{1,0:T(8,128)S(1)}, ...), condition=%wide.region_3.4_spmd.clone, body=%wide.region_2.3_spmd.clone.sunk | while | flops 293609472 | bytes 30050948 | solution.py:98
  105.8 3.6 fusion.101
  109.5 11.1 %fusion.102 = f32[1,8,32,1]{2,0,3,1:T(1,128)S(1)} fusion(f32[128,32,1,1]{0,2,1,3:T(1,128)S(1)} %copy.35, f32[8,128,32,32]{1,3,2,0:T(8,128)} %fusion.101), kind=kOutput, calls=%fused_computation.clone.1 | convolution fusion | flops 12582912 | bytes 4211712 | tf_op jit(solution)/shard_map/while/body/eval_jaxpr/ijkl,jl->ik/dot_general | solution.py:94
  120.6 4.7 fusion.103
  125.4 3.6 fusion.101
  129.1 11.1 %fusion.102 = f32[1,8,32,1]{2,0,3,1:T(1,128)S(1)} fusion(f32[128,32,1,1]{0,2,1,3:T(1,128)S(1)} %copy.35, f32[8,128,32,32]{1,3,2,0:T(8,128)} %fusion.101), kind=kOutput, calls=%fused_computation.clone.1 | convolution fusion | flops 12582912 | bytes 4211712 | tf_op jit(solution)/shard_map/while/body/eval_jaxpr/ijkl,jl->ik/dot_general | solution.py:94
  140.2 4.7 fusion.103
  145.0 3.6 fusion.101
  148.7 11.1 %fusion.102 = f32[1,8,32,1]{2,0,3,1:T(1,128)S(1)} fusion(f32[128,32,1,1]{0,2,1,3:T(1,128)S(1)} %copy.35, f32[8,128,32,32]{1,3,2,0:T(8,128)} %fusion.101), kind=kOutput, calls=%fused_computation.clone.1 | convolution fusion | flops 12582912 | bytes 4211712 | tf_op jit(solution)/shard_map/while/body/eval_jaxpr/ijkl,jl->ik/dot_general | solution.py:94
  159.8 4.7 fusion.103
  164.6 3.6 fusion.101
  168.3 11.1 %fusion.102 = f32[1,8,32,1]{2,0,3,1:T(1,128)S(1)} fusion(f32[128,32,1,1]{0,2,1,3:T(1,128)S(1)} %copy.35, f32[8,128,32,32]{1,3,2,0:T(8,128)} %fusion.101), kind=kOutput, calls=%fused_computation.clone.1 | convolution fusion | flops 12582912 | bytes 4211712 | tf_op jit(solution)/shard_map/while/body/eval_jaxpr/ijkl,jl->ik/dot_general | solution.py:94
  179.4 4.7 fusion.103
  184.2 2.0 broadcast_in_dim.16
  186.2 0.9 convolution_dynamic-update-slice_fusion
  187.1 2.5 fusion.19
  190.9 0.8 dynamic_slice.19
  191.7 143.6 %reduce-scatter.4.cloned.1.call-done = f32[8,1536]{1,0:T(8,128)} async-done(((f32[512,1536]{1,0:T(8,128)}), f32[8,1536]{1,0:T(8,128)}) %reduce-scatter.4.cloned.1.call-update) | async-done | bytes 49168 | tf_op jit(solution)/shard_map/reduce_scatter | solution.py:118
  335.3 0.9 multiply_reduce_fusion
  336.2 2.7 convolution_multiply_fusion
  339.0 3.7 fusion.15
  342.7 12.6 %fusion.70 = f32[3840,768]{1,0:T(8,128)} fusion(bf16[1024,3840]{1,0:T(8,128)(2,1)} %copy-done.6, bf16[1024,768]{1,0:T(8,128)(2,1)S(1)} %fusion.15), kind=kOutput, calls=%fused_computation.110 | convolution fusion | flops 6039797760 | bytes 21233664 | tf_op jit(solution)/shard_map/dot_general | solution.py:145
  355.3 1.3 collective-permute-start.2
  356.6 201.8 %fusion = f32[64,768]{1,0:T(8,128)S(1)} fusion(f32[3840,768]{1,0:T(8,128)} %fusion.70), kind=kCustom, calls=%all-reduce-scatter | all-reduce-scatter fusion | flops 3145729 | bytes 11993600
  558.4 1.4 collective-permute-start.4
  559.8 1.3 collective-permute-start.5
  561.1 2.0 collective-permute-start.6
  563.1 1.3 collective-permute-start.7
  564.4 1.3 collective-permute-start.3
  565.8 1.9 fusion.25
  569.0 0.6 slice-done.3
  569.6 7.4 fusion.36
  577.0 0.7 copy-done.9
  577.7 0.7 copy-done.8
  578.4 4.3 concatenate.26
  582.7 1.4 fusion.42
  584.2 323.5 %psum.14 = f32[32,128]{1,0:T(8,128)S(1)} all-reduce(f32[32,128]{1,0:T(8,128)S(1)} %fusion.60), channel_id=1, replica_groups=mesh['seq'=16,'col'=4,'batch'=2] {'seq','col'}, use_global_device_ids=true, to_apply=%region_7.8 | all-reduce | flops 4096 | bytes 32768 | tf_op jit(solution)/shard_map/psum | solution.py:157
  909.0 9.2 psum.15
  (96 shorter events, 7.8 us)
Async XLA Ops:
  7.2 22.7 %copy-start = (bf16[768,1536]{1,0:T(8,128)(2,1)S(1)}, bf16[768,1536]{1,0:T(8,128)(2,1)}, u32[]{:S(2)}) copy-start(bf16[768,1536]{1,0:T(8,128)(2,1)} %param.17) | copy-start | bytes 7077892
  7.2 96.2 %all-gather.2.cloned.1.call-start = ((), (), s32[]{:S(2)}) async-start(), calls=%async_computation.1 | async-start | bytes 1597440 | tf_op jit(solution)/shard_map/all_gather | solution.py:72
  11.8 4.7 collective-permute-start
  15.2 5.5 collective-permute-start.1
  16.5 4.9 slice-start
  17.3 4.2 slice-start.1
  17.4 4.1 copy-start.11
  21.5 8.4 copy-start.6
  21.5 9.0 copy-start.10
  21.5 81.9 %copy-start.5 = (bf16[1536,64]{0,1:T(8,128)(2,1)S(1)}, bf16[1536,64]{0,1:T(8,128)(2,1)}, u32[]{:S(2)}) copy-start(bf16[1536,64]{0,1:T(8,128)(2,1)} %param.19) | copy-start | bytes 589828
  29.9 75.9 %copy-start.4 = (bf16[1024,128]{1,0:T(8,128)(2,1)S(1)}, bf16[1024,128]{1,0:T(8,128)(2,1)}, u32[]{:S(2)}) copy-start(bf16[1024,128]{1,0:T(8,128)(2,1)} %param.20) | copy-start | bytes 786436
  31.2 304.1 %reduce-scatter.4.cloned.1.call-start = ((), (), s32[]{:S(2)}) async-start(), calls=%async_computation.2 | async-start | bytes 3194880 | tf_op jit(solution)/shard_map/reduce_scatter | solution.py:118
  109.5 11.1 %copy-start.1 = (f32[8,128,32,32]{1,3,2,0:T(8,128)S(1)}, f32[8,128,32,32]{1,3,2,0:T(8,128)}, u32[]{:S(2)}) copy-start(f32[8,128,32,32]{1,3,2,0:T(8,128)} %fusion.101) | copy-start | bytes 12582916 | tf_op jit(solution)/shard_map/while
  129.1 11.1 %copy-start.1 = (f32[8,128,32,32]{1,3,2,0:T(8,128)S(1)}, f32[8,128,32,32]{1,3,2,0:T(8,128)}, u32[]{:S(2)}) copy-start(f32[8,128,32,32]{1,3,2,0:T(8,128)} %fusion.101) | copy-start | bytes 12582916 | tf_op jit(solution)/shard_map/while
  148.7 11.1 %copy-start.1 = (f32[8,128,32,32]{1,3,2,0:T(8,128)S(1)}, f32[8,128,32,32]{1,3,2,0:T(8,128)}, u32[]{:S(2)}) copy-start(f32[8,128,32,32]{1,3,2,0:T(8,128)} %fusion.101) | copy-start | bytes 12582916 | tf_op jit(solution)/shard_map/while
  168.3 11.1 %copy-start.1 = (f32[8,128,32,32]{1,3,2,0:T(8,128)S(1)}, f32[8,128,32,32]{1,3,2,0:T(8,128)}, u32[]{:S(2)}) copy-start(f32[8,128,32,32]{1,3,2,0:T(8,128)} %fusion.101) | copy-start | bytes 12582916 | tf_op jit(solution)/shard_map/while
  186.2 3.4 copy-start.12
  342.7 12.6 %copy-start.2 = (bf16[1024,768]{1,0:T(8,128)(2,1)}, bf16[1024,768]{1,0:T(8,128)(2,1)S(1)}, u32[]{:S(2)}) copy-start(bf16[1024,768]{1,0:T(8,128)(2,1)S(1)} %fusion.15) | copy-start | bytes 4718596
  355.3 209.1 %collective-permute-start.2 = (bf16[2,768]{1,0:T(2,128)(2,1)S(1)}, bf16[2,768]{1,0:T(2,128)(2,1)S(1)}, u32[]{:S(2)}, u32[]{:S(2)}) collective-permute-start(bf16[2,768]{1,0:T(2,128)(2,1)S(1)} %get-tuple-element.104), channel_id=1, source_target_pairs={{2,0},{4,2},{6,4},{8,6},{10,8},{12,10},{14,12},{16,14},{18,16},{20... | collective-permute-start | bytes 9224 | tf_op jit(solution)/shard_map/ppermute | solution.py:23
  558.3 9.3 %copy-start.3 = (bf16[1024,768]{1,0:T(8,128)(2,1)S(1)}, bf16[1024,768]{1,0:T(8,128)(2,1)}, u32[]{:S(2)}) copy-start(bf16[1024,768]{1,0:T(8,128)(2,1)} %copy-done.2) | copy-start | bytes 4718596
  558.4 18.6 %collective-permute-start.4 = (f32[64,768]{1,0:T(8,128)S(1)}, f32[64,768]{1,0:T(8,128)S(1)}, u32[]{:S(2)}, u32[]{:S(2)}) collective-permute-start(f32[64,768]{1,0:T(8,128)S(1)} %fusion), channel_id=1, source_target_pairs={{0,2},{2,4},{4,6},{6,8},{8,10},{10,12},{12,14},{14,16},{16,18},{18... | collective-permute-start | bytes 589832
  559.8 17.2 %collective-permute-start.5 = (f32[64,768]{1,0:T(8,128)S(1)}, f32[64,768]{1,0:T(8,128)S(1)}, u32[]{:S(2)}, u32[]{:S(2)}) collective-permute-start(f32[64,768]{1,0:T(8,128)S(1)} %fusion), channel_id=1, source_target_pairs={{0,4},{2,6},{4,8},{6,10},{8,12},{10,14},{12,16},{14,18},{16,20},{1... | collective-permute-start | bytes 589832
  561.1 17.3 %collective-permute-start.6 = (f32[64,768]{1,0:T(8,128)S(1)}, f32[64,768]{1,0:T(8,128)}, u32[]{:S(2)}, u32[]{:S(2)}) collective-permute-start(f32[64,768]{1,0:T(8,128)S(1)} %fusion), channel_id=1, source_target_pairs={{0,6},{2,8},{4,10},{6,12},{8,14},{10,16},{12,18},{14,20},{16,22},{... | collective-permute-start | bytes 589832
  563.1 13.9 %collective-permute-start.7 = (f32[60,768]{1,0:T(8,128)S(1)}, f32[60,768]{1,0:T(8,128)S(1)}, u32[]{:S(2)}, u32[]{:S(2)}) collective-permute-start(f32[60,768]{1,0:T(8,128)S(1)} %slice.78), channel_id=1, source_target_pairs={{0,8},{2,10},{4,12},{6,14},{8,16},{10,18},{12,20},{14,22},{16,24},... | collective-permute-start | bytes 552968
  564.4 3.8 collective-permute-start.3
  565.7 3.2 slice-start.2
  568.1 1.5 slice-start.3
  577.0 0.7 copy-start.9
  577.0 0.7 copy-start.7
  577.7 0.7 copy-start.8
Sparse Core Ops, SparseCore 0:
  31.3 72.0 all-gather.1
  189.8 145.4 reduce-scatter.3
where the time goes:
time: 927 us; the launch traced here: 926 us
  blocking collectives  535 us (58%)
  waiting for transfers between devices  219 us (24%)
  matrix products  118 us (13%)
  between operations  15.9 us (2%)
  starting transfers between devices  13.6 us (1%)
  other arithmetic  13 us (1%)
  local copies, waits for them, and re-layouts  11.9 us (1%)
    psum x1, blocking collectives, shards(): lax.psum(jnp.dot(member, projected, precision=highest), ('seq', 'col'))  324 us
    unnamed x1, blocking collectives  202 us
    reduce_scatter x1, waiting for transfers between devices, shards(): lax.psum_scatter(placed, ('seq', 'col'), scatter_dimension=0, tiled=True)  144 us
    all_gather x1, waiting for transfers between devices, shards(): every = lax.all_gather(normed, ('seq', 'col'), axis=0, tiled=True)  72 us
    dot_general x4, matrix products, pair_step(): jnp.einsum('ijkl,jl->ik', outer_grad, right_wide, precision=highest)  44.3 us
    dot_general x4, matrix products, pair_step(): jnp.einsum('ijkl,ik->jl', outer_grad, rows_left, precision=highest)  18.7 us
  transfers between devices with their start and end apart: 10, of which 3 were waited for; matrix products, arithmetic and copies ran while one was open for 23% of the time, Pallas kernels for 0%

commit v1 on v0

--- a/solution.py
+++ b/solution.py
@@ -154,7 +154,7 @@
     )
     projected = jnp.dot(share, projection, precision=highest)
     member = (labels[None, :] == jnp.arange(BUCKETS, dtype=jnp.int32)[:, None]).astype(jnp.float32)
-    sketch = lax.psum(jnp.dot(member, projected, precision=highest), ("seq", "col"))
+    sketch = lax.psum(lax.psum(jnp.dot(member, projected, precision=highest), "col"), "seq")
     unit = sketch * lax.rsqrt(jnp.mean(sketch * sketch) + 1e-06)
     center = lax.psum(unit, "batch") / lax.axis_size("batch")
     return (input_grad[None], (unit - center)[None])

time: 927 us -> 685 us (0.74)
  blocking collectives: 535 us -> 292 us
    psum x1 -> x2, blocking collectives: 324 us -> 80.3 us  [the longest x1 65.6 us: shards(): lax.psum(lax.psum(jnp.dot(member, projected, precision=highest), 'col'),...]
  transfers between devices with their start and end apart: 10 -> 10, of which waited for: 3 -> 3; matrix products, arithmetic and copies ran while one was open for 23% -> 31% of each run, Pallas kernels for 0% -> 0%
where the time goes in v1:
time: 685 us; the launch traced here: 684 us
  blocking collectives  292 us (43%)
  waiting for transfers between devices  219 us (32%)
  matrix products  118 us (17%)
  between operations  15.9 us (2%)
  starting transfers between devices  14.4 us (2%)
  other arithmetic  13 us (2%)
  local copies, waits for them, and re-layouts  11.9 us (2%)
    unnamed x1, blocking collectives  202 us
    reduce_scatter x1, waiting for transfers between devices, shards(): lax.psum_scatter(placed, ('seq', 'col'), scatter_dimension=0, tiled=True)  144 us
    all_gather x1, waiting for transfers between devices, shards(): every = lax.all_gather(normed, ('seq', 'col'), axis=0, tiled=True)  72 us
    psum x1, blocking collectives, shards(): lax.psum(lax.psum(jnp.dot(member, projected, precision=highest), 'col'),...  65.6 us
    dot_general x4, matrix products, pair_step(): jnp.einsum('ijkl,jl->ik', outer_grad, right_wide, precision=highest)  44.3 us
    dot_general x4, matrix products, pair_step(): jnp.einsum('ijkl,ik->jl', outer_grad, rows_left, precision=highest)  18.7 us
    psum x1, blocking collectives, shards(): lax.psum(jnp.dot(member, projected, precision=highest), 'col')  14.7 us
    dot_general x4, matrix products, pair_step(): lax.dot_general(block.reshape(bins_dev * col_len, pair_channels), out_wei...  14.5 us
  transfers between devices with their start and end apart: 10, of which 3 were waited for; matrix products, arithmetic and copies ran while one was open for 31% of the time, Pallas kernels for 0%

profile of v1, /device:TPU:8, one launch (start us, length us, event | category | flops | bytes accessed | tf_op | source)
XLA Modules:
  0.0 683.7 jit_solution(6203796340050147247)
XLA Ops:
  7.7 1.8 reduce.3
  10.2 1.6 convolution_convert_fusion
  11.8 3.4 collective-permute-start
  15.2 1.3 collective-permute-start.1
  17.4 3.3 collective-permute-done.1
  21.5 8.4 %bitcast_reduce_fusion = (f32[8,768]{1,0:T(8,128)S(1)}, f32[1024,768]{1,0:T(8,128)}) fusion(f32[768]{0:T(1024)S(1)} %copy-done.11, bf16[1024,3840]{1,0:T(8,128)(2,1)S(1)} %fusion.34, bf16[3840,768]{1,0:T(8,128)(2,1)S(1)} %bitcast.117), kind=kOutput, calls=%fused_computation.26 | convolution fusion | flops 6047655936 | bytes 16935936 | tf_op jit(solution)/shard_map/dot_general | solution.py:59
  30.4 0.7 multiply_convert_fusion
  31.4 72.0 %all-gather.2.cloned.1.call-done = bf16[512,1536]{1,0:T(8,128)(2,1)} async-done(((bf16[8,1536]{1,0:T(8,128)(2,1)}), bf16[512,1536]{1,0:T(8,128)(2,1)}) %all-gather.2.cloned.1.call-update) | async-done | bytes 1572880 | tf_op jit(solution)/shard_map/all_gather | solution.py:72
  103.4 1.2 fusion.37
  104.8 1.0 fusion.39
  105.8 78.4 %while.13 = (s32[]{:T(128)}, f32[128,32]{1,0:T(8,128)S(1)}, f32[4,8,32]{2,1,0:T(8,128)S(1)}, bf16[4,8,128,128]{3,2,1,0:T(8,128)(2,1)}, bf16[1024,128]{1,0:T(8,12...) while((s32[]{:T(128)}, f32[128,32]{1,0:T(8,128)S(1)}, ...), condition=%wide.region_3.4_spmd.clone, body=%wide.region_2.3_spmd.clone.sunk | while | flops 293609472 | bytes 30050948 | solution.py:98
  105.8 3.6 fusion.101
  109.5 11.1 %fusion.102 = f32[1,8,32,1]{2,0,3,1:T(1,128)S(1)} fusion(f32[128,32,1,1]{0,2,1,3:T(1,128)S(1)} %copy.35, f32[8,128,32,32]{1,3,2,0:T(8,128)} %fusion.101), kind=kOutput, calls=%fused_computation.clone.1 | convolution fusion | flops 12582912 | bytes 4211712 | tf_op jit(solution)/shard_map/while/body/eval_jaxpr/ijkl,jl->ik/dot_general | solution.py:94
  120.6 4.7 fusion.103
  125.4 3.6 fusion.101
  129.1 11.1 %fusion.102 = f32[1,8,32,1]{2,0,3,1:T(1,128)S(1)} fusion(f32[128,32,1,1]{0,2,1,3:T(1,128)S(1)} %copy.35, f32[8,128,32,32]{1,3,2,0:T(8,128)} %fusion.101), kind=kOutput, calls=%fused_computation.clone.1 | convolution fusion | flops 12582912 | bytes 4211712 | tf_op jit(solution)/shard_map/while/body/eval_jaxpr/ijkl,jl->ik/dot_general | solution.py:94
  140.2 4.7 fusion.103
  145.0 3.6 fusion.101
  148.7 11.1 %fusion.102 = f32[1,8,32,1]{2,0,3,1:T(1,128)S(1)} fusion(f32[128,32,1,1]{0,2,1,3:T(1,128)S(1)} %copy.35, f32[8,128,32,32]{1,3,2,0:T(8,128)} %fusion.101), kind=kOutput, calls=%fused_computation.clone.1 | convolution fusion | flops 12582912 | bytes 4211712 | tf_op jit(solution)/shard_map/while/body/eval_jaxpr/ijkl,jl->ik/dot_general | solution.py:94
  159.8 4.7 fusion.103
  164.6 3.6 fusion.101
  168.3 11.1 %fusion.102 = f32[1,8,32,1]{2,0,3,1:T(1,128)S(1)} fusion(f32[128,32,1,1]{0,2,1,3:T(1,128)S(1)} %copy.35, f32[8,128,32,32]{1,3,2,0:T(8,128)} %fusion.101), kind=kOutput, calls=%fused_computation.clone.1 | convolution fusion | flops 12582912 | bytes 4211712 | tf_op jit(solution)/shard_map/while/body/eval_jaxpr/ijkl,jl->ik/dot_general | solution.py:94
  179.4 4.7 fusion.103
  184.2 2.0 broadcast_in_dim.16
  186.2 0.9 convolution_dynamic-update-slice_fusion
  187.1 2.5 fusion.19
  190.9 0.8 dynamic_slice.19
  191.6 143.6 %reduce-scatter.4.cloned.1.call-done = f32[8,1536]{1,0:T(8,128)} async-done(((f32[512,1536]{1,0:T(8,128)}), f32[8,1536]{1,0:T(8,128)}) %reduce-scatter.4.cloned.1.call-update) | async-done | bytes 49168 | tf_op jit(solution)/shard_map/reduce_scatter | solution.py:118
  335.3 0.9 multiply_reduce_fusion
  336.2 2.7 convolution_multiply_fusion
  338.9 3.7 fusion.15
  342.6 12.6 %fusion.70 = f32[3840,768]{1,0:T(8,128)} fusion(bf16[1024,3840]{1,0:T(8,128)(2,1)} %copy-done.6, bf16[1024,768]{1,0:T(8,128)(2,1)S(1)} %fusion.15), kind=kOutput, calls=%fused_computation.110 | convolution fusion | flops 6039797760 | bytes 21233664 | tf_op jit(solution)/shard_map/dot_general | solution.py:145
  355.3 1.3 collective-permute-start.2
  356.6 201.8 %fusion = f32[64,768]{1,0:T(8,128)S(1)} fusion(f32[3840,768]{1,0:T(8,128)} %fusion.70), kind=kCustom, calls=%all-reduce-scatter | all-reduce-scatter fusion | flops 3145729 | bytes 11993600
  558.4 1.7 collective-permute-start.4
  560.0 1.3 collective-permute-start.5
  561.3 2.0 collective-permute-start.6
  563.3 1.3 collective-permute-start.7
  564.6 1.9 collective-permute-start.3
  566.6 1.9 fusion.25
  570.4 7.4 %fusion.36 = bf16[1,1024,768]{2,1,0:T(8,128)(2,1)} fusion(bf16[1024,5,768]{2,0,1:T(8,128)(2,1)S(1)} %fusion.31, bf16[5,768,768]{2,1,0:T(8,128)(2,1)S(1)} %bitcast.120), kind=kOutput, calls=%fused_computation.61 | convolution fusion | flops 6040584192 | bytes 15335424 | tf_op jit(solution)/shard_map/tko,kio->ti/dot_general | solution.py:137
  577.8 0.7 copy-done.9
  578.5 0.7 copy-done.8
  579.2 4.3 concatenate.26
  583.5 1.4 fusion.42
  585.0 14.7 %psum.21 = f32[32,128]{1,0:T(8,128)S(1)} all-reduce(f32[32,128]{1,0:T(8,128)S(1)} %fusion.60), channel_id=1, replica_groups=mesh['seq'=16,'col'=4,'batch'=2] {'col'}, use_global_device_ids=true, to_apply=%region_7.8 | all-reduce | flops 4096 | bytes 32768 | tf_op jit(solution)/shard_map/psum | solution.py:157
  599.7 65.6 %psum.22 = f32[32,128]{1,0:T(8,128)S(1)} all-reduce(f32[32,128]{1,0:T(8,128)S(1)} %psum.21), channel_id=1, replica_groups=mesh['seq'=16,'col'=4,'batch'=2] {'seq'}, use_global_device_ids=true, to_apply=%region_8.9 | all-reduce | flops 4096 | bytes 32768 | tf_op jit(solution)/shard_map/psum | solution.py:157
  666.5 9.8 %psum.23 = f32[32,128]{1,0:T(8,128)S(1)} all-reduce(f32[32,128]{1,0:T(8,128)S(1)} %broadcast_multiply_fusion), channel_id=1, replica_groups=mesh['seq'=16,'col'=4,'batch'=2] {'batch'}, use_global_device_ids=true, to_apply=%region_10.11 | all-reduce | flops 4096 | bytes 32768 | tf_op jit(solution)/shard_map/psum | solution.py:159
  (97 shorter events, 8.4 us)
Async XLA Ops:
  7.2 22.7 %copy-start = (bf16[768,1536]{1,0:T(8,128)(2,1)S(1)}, bf16[768,1536]{1,0:T(8,128)(2,1)}, u32[]{:S(2)}) copy-start(bf16[768,1536]{1,0:T(8,128)(2,1)} %param.17) | copy-start | bytes 7077892
  7.2 96.2 %all-gather.2.cloned.1.call-start = ((), (), s32[]{:S(2)}) async-start(), calls=%async_computation.1 | async-start | bytes 1597440 | tf_op jit(solution)/shard_map/all_gather | solution.py:72
  11.8 4.7 collective-permute-start
  15.2 5.5 collective-permute-start.1
  16.5 4.9 slice-start
  17.3 4.2 slice-start.1
  17.4 4.1 copy-start.11
  21.5 8.4 %copy-start.6 = (bf16[1024,3840]{1,0:T(8,128)(2,1)}, bf16[1024,3840]{1,0:T(8,128)(2,1)S(1)}, u32[]{:S(2)}) copy-start(bf16[1024,3840]{1,0:T(8,128)(2,1)S(1)} %fusion.34) | copy-start | bytes 23592964
  21.5 9.0 %copy-start.10 = (f32[1536]{0:T(1024)S(1)}, f32[1536]{0:T(1024)}, u32[]{:S(2)}) copy-start(f32[1536]{0:T(1024)} %param.18) | copy-start | bytes 18436
  21.5 81.9 %copy-start.5 = (bf16[1536,64]{0,1:T(8,128)(2,1)S(1)}, bf16[1536,64]{0,1:T(8,128)(2,1)}, u32[]{:S(2)}) copy-start(bf16[1536,64]{0,1:T(8,128)(2,1)} %param.19) | copy-start | bytes 589828
  29.9 75.9 %copy-start.4 = (bf16[1024,128]{1,0:T(8,128)(2,1)S(1)}, bf16[1024,128]{1,0:T(8,128)(2,1)}, u32[]{:S(2)}) copy-start(bf16[1024,128]{1,0:T(8,128)(2,1)} %param.20) | copy-start | bytes 786436
  31.2 304.1 %reduce-scatter.4.cloned.1.call-start = ((), (), s32[]{:S(2)}) async-start(), calls=%async_computation.2 | async-start | bytes 3194880 | tf_op jit(solution)/shard_map/reduce_scatter | solution.py:118
  109.5 11.1 %copy-start.1 = (f32[8,128,32,32]{1,3,2,0:T(8,128)S(1)}, f32[8,128,32,32]{1,3,2,0:T(8,128)}, u32[]{:S(2)}) copy-start(f32[8,128,32,32]{1,3,2,0:T(8,128)} %fusion.101) | copy-start | bytes 12582916 | tf_op jit(solution)/shard_map/while
  129.1 11.1 %copy-start.1 = (f32[8,128,32,32]{1,3,2,0:T(8,128)S(1)}, f32[8,128,32,32]{1,3,2,0:T(8,128)}, u32[]{:S(2)}) copy-start(f32[8,128,32,32]{1,3,2,0:T(8,128)} %fusion.101) | copy-start | bytes 12582916 | tf_op jit(solution)/shard_map/while
  148.7 11.1 %copy-start.1 = (f32[8,128,32,32]{1,3,2,0:T(8,128)S(1)}, f32[8,128,32,32]{1,3,2,0:T(8,128)}, u32[]{:S(2)}) copy-start(f32[8,128,32,32]{1,3,2,0:T(8,128)} %fusion.101) | copy-start | bytes 12582916 | tf_op jit(solution)/shard_map/while
  168.3 11.1 %copy-start.1 = (f32[8,128,32,32]{1,3,2,0:T(8,128)S(1)}, f32[8,128,32,32]{1,3,2,0:T(8,128)}, u32[]{:S(2)}) copy-start(f32[8,128,32,32]{1,3,2,0:T(8,128)} %fusion.101) | copy-start | bytes 12582916 | tf_op jit(solution)/shard_map/while
  186.2 3.4 copy-start.12
  342.6 12.6 %copy-start.2 = (bf16[1024,768]{1,0:T(8,128)(2,1)}, bf16[1024,768]{1,0:T(8,128)(2,1)S(1)}, u32[]{:S(2)}) copy-start(bf16[1024,768]{1,0:T(8,128)(2,1)S(1)} %fusion.15) | copy-start | bytes 4718596
  355.3 209.4 %collective-permute-start.2 = (bf16[2,768]{1,0:T(2,128)(2,1)S(1)}, bf16[2,768]{1,0:T(2,128)(2,1)S(1)}, u32[]{:S(2)}, u32[]{:S(2)}) collective-permute-start(bf16[2,768]{1,0:T(2,128)(2,1)S(1)} %get-tuple-element.104), channel_id=1, source_target_pairs={{2,0},{4,2},{6,4},{8,6},{10,8},{12,10},{14,12},{16,14},{18,16},{20... | collective-permute-start | bytes 9224 | tf_op jit(solution)/shard_map/ppermute | solution.py:23
  558.3 10.2 %copy-start.3 = (bf16[1024,768]{1,0:T(8,128)(2,1)S(1)}, bf16[1024,768]{1,0:T(8,128)(2,1)}, u32[]{:S(2)}) copy-start(bf16[1024,768]{1,0:T(8,128)(2,1)} %copy-done.2) | copy-start | bytes 4718596
  558.4 19.4 %collective-permute-start.4 = (f32[64,768]{1,0:T(8,128)S(1)}, f32[64,768]{1,0:T(8,128)S(1)}, u32[]{:S(2)}, u32[]{:S(2)}) collective-permute-start(f32[64,768]{1,0:T(8,128)S(1)} %fusion), channel_id=1, source_target_pairs={{0,2},{2,4},{4,6},{6,8},{8,10},{10,12},{12,14},{14,16},{16,18},{18... | collective-permute-start | bytes 589832
  560.0 17.8 %collective-permute-start.5 = (f32[64,768]{1,0:T(8,128)S(1)}, f32[64,768]{1,0:T(8,128)S(1)}, u32[]{:S(2)}, u32[]{:S(2)}) collective-permute-start(f32[64,768]{1,0:T(8,128)S(1)} %fusion), channel_id=1, source_target_pairs={{0,4},{2,6},{4,8},{6,10},{8,12},{10,14},{12,16},{14,18},{16,20},{1... | collective-permute-start | bytes 589832
  561.3 17.9 %collective-permute-start.6 = (f32[64,768]{1,0:T(8,128)S(1)}, f32[64,768]{1,0:T(8,128)}, u32[]{:S(2)}, u32[]{:S(2)}) collective-permute-start(f32[64,768]{1,0:T(8,128)S(1)} %fusion), channel_id=1, source_target_pairs={{0,6},{2,8},{4,10},{6,12},{8,14},{10,16},{12,18},{14,20},{16,22},{... | collective-permute-start | bytes 589832
  563.3 14.5 %collective-permute-start.7 = (f32[60,768]{1,0:T(8,128)S(1)}, f32[60,768]{1,0:T(8,128)S(1)}, u32[]{:S(2)}, u32[]{:S(2)}) collective-permute-start(f32[60,768]{1,0:T(8,128)S(1)} %slice.78), channel_id=1, source_target_pairs={{0,8},{2,10},{4,12},{6,14},{8,16},{10,18},{12,20},{14,22},{16,24},... | collective-permute-start | bytes 552968
  564.6 4.4 collective-permute-start.3
  566.5 3.2 slice-start.2
  568.9 1.5 slice-start.3
  577.8 0.7 copy-start.9
  577.8 0.7 copy-start.7
  578.5 0.7 copy-start.8
Sparse Core Ops, SparseCore 0:
  31.3 72.0 all-gather.1
  189.7 145.5 reduce-scatter.3
